TPU v7x, 256 devices: a whole 4x4x8 slice. The times are simulated.
256 devices in a mesh: grp: 4 (over x), dev: 64 (over z, y, core).
Axes of the slice: x: 4, y: 4, z: 8, core: 2. Of those that a mesh axis runs over, the one named last changes fastest.
Arguments:
- node_feat: bfloat16 [524288, 256], P(('grp', 'dev')), may hold values from -6 to 6
- send_node: int32 [256, 256, 16], P(('grp', 'dev')), may hold values from 0 to 2047, as said below
- pin_net: int32 [256, 256, 16], P(('grp', 'dev')), may hold values from 0 to 1023, as said below
- pin_count: int32 [256, 256], P(('grp', 'dev')), may hold values from 4 to 16, as said below
- pin_w1: bfloat16 [256, 512], replicated, may hold values from -0.375 to 0.375
- pin_b1: float32 [512], replicated, may hold values from -4 to 4
- pin_w2: bfloat16 [512, 256], replicated, may hold values from -0.25 to 0.25
- net_w1: bfloat16 [256, 512], replicated, may hold values from -0.375 to 0.375
- net_b1: float32 [512], replicated, may hold values from -4 to 4
- net_w2: bfloat16 [512, 256], replicated, may hold values from -0.25 to 0.25
- self_w: bfloat16 [256, 512], replicated, may hold values from -0.375 to 0.375
- msg_w: bfloat16 [256, 512], replicated, may hold values from -0.375 to 0.375
- node_b: float32 [512], replicated, may hold values from -4 to 4
- out_w: bfloat16 [512, 256], replicated, may hold values from -0.25 to 0.25
Outputs:
- updated: bfloat16 [524288, 256], P(('grp', 'dev'))
Inputs may be any that keep to these rules, and one draw needn't show every extreme that they name: `send_node`: slots at or past the count hold arbitrary local nodes. `pin_net`: every net of every owner has at least one live pin; slots at or past the count hold arbitrary local nets. `pin_count`: in every draw each net owner receives 16 live slots from some device, and some net owner receives 16 live slots from every device.
All inputs are finite; a program needn't handle non-finite values.
Results may differ from a plain program's by a relative error of at most 0.0055.
Values may be sent and summed in bfloat16 or wider, within the bound.
A program may use at most 64 MiB of HBM per device.

v0:
```python
import math

import jax
import jax.numpy as jnp
from jax import lax
from jax.sharding import PartitionSpec as P

NET_DEV = 1024


def pin_transform(node_rows, pin_w1, pin_b1, pin_w2):
    hidden_act = jax.nn.gelu(
        jnp.dot(node_rows, pin_w1, preferred_element_type=jnp.float32) + pin_b1
    )
    return jnp.dot(
        hidden_act.astype(jnp.bfloat16), pin_w2, preferred_element_type=jnp.float32
    ).astype(jnp.bfloat16)


def onehot_sums(targets, rows, width):
    total_rows = rows.shape[0]
    feat_width = rows.shape[1]
    block_rows = math.gcd(total_rows, 512)
    block_count = total_rows // block_rows
    target_blocks = targets.reshape(block_count, block_rows)
    row_blocks = rows.reshape(block_count, block_rows, feat_width)
    column_ids = lax.broadcasted_iota(jnp.int32, (1, width), 1)

    def add_block(carry, inputs):
        sums_now, sizes_now = carry
        block_targets, block_values = inputs
        selector = (block_targets[:, None] == column_ids).astype(jnp.bfloat16)
        added = lax.dot_general(
            selector, block_values, (((0,), (0,)), ((), ())), preferred_element_type=jnp.float32
        )
        sizes_next = sizes_now + jnp.sum(selector, axis=0, dtype=jnp.float32)
        return ((sums_now + added, sizes_next), None)

    start = (jnp.zeros((width, feat_width), jnp.float32), jnp.zeros((width,), jnp.float32))
    (sums_out, sizes_out), _ = lax.scan(add_block, start, (target_blocks, row_blocks))
    return (sums_out, sizes_out)


def shards(
    node_feat,
    send_node,
    pin_net,
    pin_count,
    pin_w1,
    pin_b1,
    pin_w2,
    net_w1,
    net_b1,
    net_w2,
    self_w,
    msg_w,
    node_b,
    out_w,
):
    groups = lax.axis_size("grp")
    members = lax.axis_size("dev")
    slot_count = send_node.shape[2]
    feat_width = node_feat.shape[1]
    node_picks = send_node.reshape(-1)
    pin_feat = pin_transform(node_feat, pin_w1, pin_b1, pin_w2)
    outgoing = jnp.take(pin_feat, node_picks, axis=0).reshape(
        groups, members, slot_count, feat_width
    )
    arrived = lax.all_to_all(
        lax.all_to_all(outgoing, "grp", split_axis=0, concat_axis=0, tiled=True),
        "dev",
        split_axis=1,
        concat_axis=1,
        tiled=True,
    )
    sources = pin_count.shape[1]
    live_mask = (
        lax.broadcasted_iota(jnp.int32, (sources, slot_count), 1) < pin_count.reshape(-1, 1)
    ).reshape(-1)
    net_ids = pin_net.reshape(-1)
    live_nets = jnp.where(live_mask, net_ids, -1)
    net_sums, net_sizes = onehot_sums(live_nets, arrived.reshape(-1, feat_width), NET_DEV)
    net_mean = (net_sums / net_sizes[:, None]).astype(jnp.bfloat16)
    net_inner = jax.nn.gelu(
        jnp.dot(net_mean, net_w1, preferred_element_type=jnp.float32) + net_b1
    ).astype(jnp.bfloat16)
    message = jnp.dot(net_inner, net_w2, preferred_element_type=jnp.float32).astype(jnp.bfloat16)
    per_pin = jnp.where(
        live_mask[:, None], jnp.take(message, net_ids, axis=0), jnp.zeros((), jnp.bfloat16)
    )
    returned = lax.all_to_all(
        lax.all_to_all(
            per_pin.reshape(groups, members, slot_count, feat_width),
            "grp",
            split_axis=0,
            concat_axis=0,
            tiled=True,
        ),
        "dev",
        split_axis=1,
        concat_axis=1,
        tiled=True,
    )
    node_total, _ = onehot_sums(node_picks, returned.reshape(-1, feat_width), node_feat.shape[0])
    node_sum = node_total.astype(jnp.bfloat16)
    self_part = jnp.dot(node_feat, self_w, preferred_element_type=jnp.float32)
    pre_act = self_part + jnp.dot(node_sum, msg_w, preferred_element_type=jnp.float32) + node_b
    node_inner = jax.nn.silu(pre_act).astype(jnp.bfloat16)
    return (
        node_feat.astype(jnp.float32)
        + jnp.dot(node_inner, out_w, preferred_element_type=jnp.float32)
    ).astype(jnp.bfloat16)


def solution(mesh):
    in_specs = (
        P(("grp", "dev"), None),
        P(("grp", "dev"), None, None),
        P(("grp", "dev"), None, None),
        P(("grp", "dev"), None),
        P(),
        P(),
        P(),
        P(),
        P(),
        P(),
        P(),
        P(),
        P(),
        P(),
    )
    out_specs = P(("grp", "dev"), None)
    return jax.shard_map(shards, mesh=mesh, in_specs=in_specs, out_specs=out_specs, check_vma=False)
```

profile of v0, /device:TPU:1, one launch (start us, length us, event | category | flops | bytes accessed | tf_op | source)
XLA Modules:
  0.0 287.3 jit_solution(6051878504943641346)
XLA Ops:
  0.0 0.9 copy.67
  1.7 3.1 %convolution_convert_fusion = bf16[2048,256]{1,0:T(8,128)(2,1)S(1)} fusion(bf16[512,256]{1,0:T(8,128)(2,1)} %param.24, bf16[2048,256]{1,0:T(8,128)(2,1)} %param.18, bf16[256,512]{1,0:T(8,128)(2,1)} %param.22, f32[512]{0:T(512)} %param.23), kind=kOutput, calls=%fused_computation.36 | convolution fusion | flops 1084751872 | bytes 2623488 | tf_op jit(solution)/shard_map/dot_general | solution.py:15
  4.8 14.6 %gather_fusion = bf16[4096,256]{1,0:T(8,128)(2,1)S(1)} fusion(bf16[2048,256]{1,0:T(8,128)(2,1)S(1)} %convolution_convert_fusion, s32[4096]{0:T(1024)S(1)} %broadcast_clamp_fusion.1), kind=kCustom, calls=%fused_computation | custom fusion | bytes 4210688 | tf_op jit(solution)/shard_map/jit(_take)/gather | solution.py:66
  19.4 2.0 broadcast_select_fusion
  21.5 29.9 %all_to_all.20 = bf16[4,64,16,256]{3,2,1,0:T(8,128)(2,1)S(1)} all-to-all(bf16[4,64,16,256]{3,2,1,0:T(8,128)(2,1)S(1)} %broadcast_select_fusion), channel_id=1, replica_groups=mesh['grp'=4,'dev'=64] {'grp'}, dimensions={0} | all-to-all | bytes 4194304 | tf_op jit(solution)/shard_map/all_to_all | solution.py:70
  51.4 1.6 copy.76
  53.0 13.8 %all-to-all-start.1 = ((bf16[4,64,16,256]{3,2,0,1:T(8,128)(2,1)}), bf16[4,64,16,256]{3,2,0,1:T(8,128)(2,1)S(1)}, u32[]{:S(2)}, u32[]{:S(2)}) async-start(bf16[4,64,16,256]{3,2,0,1:T(8,128)(2,1)} %copy.76), calls=%async_computation.1 | async-start | bytes 4194304 | tf_op jit(solution)/shard_map/all_to_all | solution.py:69
  70.3 0.8 iota.29
  71.1 0.8 lt.76
  71.9 1.6 lt.77
  73.5 0.7 compare_select_fusion.2
  74.8 1.3 compare_select_fusion.4
  76.2 1.6 iota_compare_fusion.8
  77.8 38.7 %all-to-all-done.1 = bf16[4,64,16,256]{3,2,0,1:T(8,128)(2,1)S(1)} async-done(((bf16[4,64,16,256]{3,2,0,1:T(8,128)(2,1)}), bf16[4,64,16,256]{3,2,0,1:T(8,128)(2,1)S(1)}, u32[]{:S(2)}, u32[]{:S(2)}) %all-to-all-start.1) | async-done | bytes 2097184 | tf_op jit(solution)/shard_map/all_to_all | solution.py:69
  116.5 1.5 copy.77
  118.0 25.7 %while.24 = (s32[]{:T(128)}, f32[1024,256]{1,0:T(8,128)S(1)}, f32[1024]{0:T(1024)S(1)}, s32[8,512]{1,0:T(8,128)}, bf16[8,512,256]{2,1,0:T(8,128)(2,1)}, /*index=5*/s32[]{:T(128)}, s32[]{:T(128)}) while((s32[]{:T(128)}, f32[1024,256]{1,0:T(8,128)S(1)}, f32[1024]{0:T(1024)S(1)}, s32[8,512]{1,0:T(8,128)}, ...), condition=%wide.region_2.3_spmd.clone, body=%wide.region_0.0_spmd.clone.sunk | while | flops 271582208 | bytes 2383976 | solution.py:40
  118.0 0.8 constant_dynamic-slice_fusion.4
  119.1 2.1 fusion.69
  121.3 0.7 constant_dynamic-slice_fusion.4
  122.3 2.2 fusion.69
  124.5 0.7 constant_dynamic-slice_fusion.4
  125.5 2.2 fusion.69
  127.7 0.7 constant_dynamic-slice_fusion.4
  128.7 2.1 fusion.69
  130.9 0.7 constant_dynamic-slice_fusion.4
  131.9 2.2 fusion.69
  135.1 2.2 fusion.69
  138.3 2.1 fusion.69
  141.5 2.2 fusion.69
  143.7 1.1 fusion.35
  144.8 16.9 %gather_fusion.1 = bf16[4096,256]{1,0:T(8,128)(2,1)} fusion(bf16[1024,256]{1,0:T(8,128)(2,1)S(1)} %fusion.35, s32[4096]{0:T(1024)S(1)} %copy-done.5), kind=kCustom, calls=%fused_computation.1 | custom fusion | bytes 4210688 | tf_op jit(solution)/shard_map/jit(_take)/gather | solution.py:89
  161.8 3.2 %select_select_fusion = bf16[4,64,16,256]{3,2,1,0:T(8,128)(2,1)S(1)} fusion(bf16[4,64,16,256]{3,2,1,0:T(8,128)(2,1)} %bitcast.34, pred[4,64,16]{2,1,0:T(8,128)(4,1)S(1)} %copy-done.4, pred[4,64,16]{2,1,0:T(8,128)(4,1)S(1)} %copy-done.3), kind=kLoop, calls=%fused_computation.45 | loop fusion | flops 2097152 | bytes 4202496 | tf_op jit(solution)/shard_map/jit(_where)/select_n | solution.py:88
  165.0 26.4 %all_to_all.21 = bf16[4,64,16,256]{3,2,1,0:T(8,128)(2,1)S(1)} all-to-all(bf16[4,64,16,256]{3,2,1,0:T(8,128)(2,1)S(1)} %select_select_fusion), channel_id=1, replica_groups=mesh['grp'=4,'dev'=64] {'grp'}, dimensions={0} | all-to-all | bytes 4194304 | tf_op jit(solution)/shard_map/all_to_all | solution.py:92
  191.4 1.7 copy.79
  193.0 10.0 %all-to-all-start.3 = ((bf16[4,64,16,256]{3,2,0,1:T(8,128)(2,1)}), bf16[4,64,16,256]{3,2,0,1:T(8,128)(2,1)}, u32[]{:S(2)}, u32[]{:S(2)}) async-start(bf16[4,64,16,256]{3,2,0,1:T(8,128)(2,1)} %copy.79), calls=%async_computation.3 | async-start | bytes 4194304 | tf_op jit(solution)/shard_map/all_to_all | solution.py:91
  203.2 2.6 fusion.54
  205.8 46.8 %all-to-all-done.3 = bf16[4,64,16,256]{3,2,0,1:T(8,128)(2,1)} async-done(((bf16[4,64,16,256]{3,2,0,1:T(8,128)(2,1)}), bf16[4,64,16,256]{3,2,0,1:T(8,128)(2,1)}, u32[]{:S(2)}, u32[]{:S(2)}) %all-to-all-start.3) | async-done | bytes 2097184 | tf_op jit(solution)/shard_map/all_to_all | solution.py:91
  252.6 3.1 %copy.80 = bf16[4,64,16,256]{3,2,1,0:T(8,128)(2,1)} copy(bf16[4,64,16,256]{3,2,0,1:T(8,128)(2,1)} %all-to-all-done.3) | data formatting | bytes 4194304 | tf_op jit(solution)/shard_map/all_to_all | solution.py:91
  255.8 26.7 %while.25 = (s32[]{:T(128)}, f32[2048,256]{1,0:T(8,128)S(1)}, s32[8,512]{1,0:T(8,128)S(1)}, bf16[8,512,256]{2,1,0:T(8,128)(2,1)}, s32[]{:T(128)}, /*index=5*/s32[]{:T(128)}) while((s32[]{:T(128)}, f32[2048,256]{1,0:T(8,128)S(1)}, s32[8,512]{1,0:T(8,128)S(1)}, bf16[8,512,256]{2,1,0:T(8,128)(2,1)}, s32[]{:T(128)}, ...), condition=%wide.region_4.5_spmd.clone, body=%wide.region_3.4_spmd.clone.sunk | while | flops 538968064 | bytes 4462687 | solution.py:40
  255.8 3.3 %fusion.71 = f32[2048,256]{1,0:T(8,128)S(1)} fusion(f32[2048,256]{1,0:T(8,128)S(1)} %get-tuple-element.209, s32[512]{0:T(512)S(1)} %bitcast.42, pred[]{:T(512)S(6)} %compare.7, bf16[8,512,256]{2,1,0:T(8,128)(2,1)} %get-tuple-element.217, s32[]{:T(128)S(6)} %copy.94), kind=kOutput, calls=%fused_computation.17.clone.1 | convolution fusion | flops 538968064 | bytes 4458501 | tf_op jit(solution)/shard_map/while/body/eval_jaxpr/dot_general | solution.py:33
  259.1 3.3 %fusion.71 = f32[2048,256]{1,0:T(8,128)S(1)} fusion(f32[2048,256]{1,0:T(8,128)S(1)} %get-tuple-element.209, s32[512]{0:T(512)S(1)} %bitcast.42, pred[]{:T(512)S(6)} %compare.7, bf16[8,512,256]{2,1,0:T(8,128)(2,1)} %get-tuple-element.217, s32[]{:T(128)S(6)} %copy.94), kind=kOutput, calls=%fused_computation.17.clone.1 | convolution fusion | flops 538968064 | bytes 4458501 | tf_op jit(solution)/shard_map/while/body/eval_jaxpr/dot_general | solution.py:33
  262.5 3.3 %fusion.71 = f32[2048,256]{1,0:T(8,128)S(1)} fusion(f32[2048,256]{1,0:T(8,128)S(1)} %get-tuple-element.209, s32[512]{0:T(512)S(1)} %bitcast.42, pred[]{:T(512)S(6)} %compare.7, bf16[8,512,256]{2,1,0:T(8,128)(2,1)} %get-tuple-element.217, s32[]{:T(128)S(6)} %copy.94), kind=kOutput, calls=%fused_computation.17.clone.1 | convolution fusion | flops 538968064 | bytes 4458501 | tf_op jit(solution)/shard_map/while/body/eval_jaxpr/dot_general | solution.py:33
  265.8 3.3 %fusion.71 = f32[2048,256]{1,0:T(8,128)S(1)} fusion(f32[2048,256]{1,0:T(8,128)S(1)} %get-tuple-element.209, s32[512]{0:T(512)S(1)} %bitcast.42, pred[]{:T(512)S(6)} %compare.7, bf16[8,512,256]{2,1,0:T(8,128)(2,1)} %get-tuple-element.217, s32[]{:T(128)S(6)} %copy.94), kind=kOutput, calls=%fused_computation.17.clone.1 | convolution fusion | flops 538968064 | bytes 4458501 | tf_op jit(solution)/shard_map/while/body/eval_jaxpr/dot_general | solution.py:33
  269.1 3.3 %fusion.71 = f32[2048,256]{1,0:T(8,128)S(1)} fusion(f32[2048,256]{1,0:T(8,128)S(1)} %get-tuple-element.209, s32[512]{0:T(512)S(1)} %bitcast.42, pred[]{:T(512)S(6)} %compare.7, bf16[8,512,256]{2,1,0:T(8,128)(2,1)} %get-tuple-element.217, s32[]{:T(128)S(6)} %copy.94), kind=kOutput, calls=%fused_computation.17.clone.1 | convolution fusion | flops 538968064 | bytes 4458501 | tf_op jit(solution)/shard_map/while/body/eval_jaxpr/dot_general | solution.py:33
  272.5 3.3 %fusion.71 = f32[2048,256]{1,0:T(8,128)S(1)} fusion(f32[2048,256]{1,0:T(8,128)S(1)} %get-tuple-element.209, s32[512]{0:T(512)S(1)} %bitcast.42, pred[]{:T(512)S(6)} %compare.7, bf16[8,512,256]{2,1,0:T(8,128)(2,1)} %get-tuple-element.217, s32[]{:T(128)S(6)} %copy.94), kind=kOutput, calls=%fused_computation.17.clone.1 | convolution fusion | flops 538968064 | bytes 4458501 | tf_op jit(solution)/shard_map/while/body/eval_jaxpr/dot_general | solution.py:33
  275.8 3.3 %fusion.71 = f32[2048,256]{1,0:T(8,128)S(1)} fusion(f32[2048,256]{1,0:T(8,128)S(1)} %get-tuple-element.209, s32[512]{0:T(512)S(1)} %bitcast.42, pred[]{:T(512)S(6)} %compare.7, bf16[8,512,256]{2,1,0:T(8,128)(2,1)} %get-tuple-element.217, s32[]{:T(128)S(6)} %copy.94), kind=kOutput, calls=%fused_computation.17.clone.1 | convolution fusion | flops 538968064 | bytes 4458501 | tf_op jit(solution)/shard_map/while/body/eval_jaxpr/dot_general | solution.py:33
  279.2 3.3 %fusion.71 = f32[2048,256]{1,0:T(8,128)S(1)} fusion(f32[2048,256]{1,0:T(8,128)S(1)} %get-tuple-element.209, s32[512]{0:T(512)S(1)} %bitcast.42, pred[]{:T(512)S(6)} %compare.7, bf16[8,512,256]{2,1,0:T(8,128)(2,1)} %get-tuple-element.217, s32[]{:T(128)S(6)} %copy.94), kind=kOutput, calls=%fused_computation.17.clone.1 | convolution fusion | flops 538968064 | bytes 4458501 | tf_op jit(solution)/shard_map/while/body/eval_jaxpr/dot_general | solution.py:33
  282.5 4.8 %fusion.25 = bf16[2048,256]{1,0:T(8,128)(2,1)} fusion(bf16[512,256]{1,0:T(8,128)(2,1)} %param.31, bf16[2048,256]{1,0:T(8,128)(2,1)S(1)} %copy-done.1, f32[2048,512]{1,0:T(8,128)} %fusion.54, bf16[256,512]{1,0:T(8,128)(2,1)} %param.29, f32[512]{0:T(512)S(1)} %copy-done.11, f32[2048,256]{1,0:T(8,128)S(1)} %get-tuple-element.67), kind=kOutput, calls=%fused_computation.35 | convolution fusion | flops 1083179008 | bytes 8914944 | tf_op jit(solution)/shard_map/dot_general | solution.py:111
  (68 shorter events, 9.5 us)
Async XLA Ops:
  0.0 203.2 %copy-start = (bf16[256,512]{1,0:T(8,128)(2,1)S(1)}, bf16[256,512]{1,0:T(8,128)(2,1)}, u32[]{:S(2)}) copy-start(bf16[256,512]{1,0:T(8,128)(2,1)} %param.28) | copy-start | bytes 786436
  53.0 13.8 %copy-start.6 = (s32[1,256,16]{1,2,0:T(8,128)S(1)}, s32[1,256,16]{1,2,0:T(8,128)}, u32[]{:S(2)}) copy-start(s32[1,256,16]{1,2,0:T(8,128)} %param.20) | copy-start | bytes 49156
  53.0 15.8 %copy-start.7 = (s32[1,256]{1,0:T(1,128)S(1)}, s32[1,256]{1,0:T(1,128)}, u32[]{:S(2)}) copy-start(s32[1,256]{1,0:T(1,128)} %param.21) | copy-start | bytes 3076
  53.0 63.5 %all-to-all-start.1 = ((bf16[4,64,16,256]{3,2,0,1:T(8,128)(2,1)}), bf16[4,64,16,256]{3,2,0,1:T(8,128)(2,1)S(1)}, u32[]{:S(2)}, u32[]{:S(2)}) async-start(bf16[4,64,16,256]{3,2,0,1:T(8,128)(2,1)} %copy.76), calls=%async_computation.1 | async-start | bytes 4194304 | tf_op jit(solution)/shard_map/all_to_all | solution.py:69
  66.9 0.7 copy-start.2
  118.0 25.7 %copy-start.8 = (bf16[512,256]{1,0:T(8,128)(2,1)S(1)}, bf16[512,256]{1,0:T(8,128)(2,1)}, u32[]{:S(2)}) copy-start(bf16[512,256]{1,0:T(8,128)(2,1)} %param.27) | copy-start | bytes 786436
  118.0 25.7 %copy-start.9 = (bf16[256,512]{1,0:T(8,128)(2,1)S(1)}, bf16[256,512]{1,0:T(8,128)(2,1)}, u32[]{:S(2)}) copy-start(bf16[256,512]{1,0:T(8,128)(2,1)} %param.25) | copy-start | bytes 786436
  118.0 25.7 %copy-start.10 = (f32[512]{0:T(512)S(1)}, f32[512]{0:T(512)}, u32[]{:S(2)}) copy-start(f32[512]{0:T(512)} %param.26) | copy-start | bytes 6148
  143.7 1.1 copy-start.5
  144.8 17.0 %copy-start.3 = (pred[4,64,16]{2,1,0:T(8,128)(4,1)S(1)}, pred[4,64,16]{2,1,0:T(8,128)(4,1)}, u32[]{:S(2)}) copy-start(pred[4,64,16]{2,1,0:T(8,128)(4,1)} %get-tuple-element.123) | copy-start | bytes 12292
  144.8 17.0 %copy-start.4 = (pred[4,64,16]{2,1,0:T(8,128)(4,1)S(1)}, pred[4,64,16]{2,1,0:T(8,128)(4,1)}, u32[]{:S(2)}) copy-start(pred[4,64,16]{2,1,0:T(8,128)(4,1)} %get-tuple-element.124) | copy-start | bytes 12292
  193.0 10.2 %copy-start.1 = (bf16[2048,256]{1,0:T(8,128)(2,1)S(1)}, bf16[2048,256]{1,0:T(8,128)(2,1)}, u32[]{:S(2)}) copy-start(bf16[2048,256]{1,0:T(8,128)(2,1)} %param.18) | copy-start | bytes 3145732
  193.0 59.6 %all-to-all-start.3 = ((bf16[4,64,16,256]{3,2,0,1:T(8,128)(2,1)}), bf16[4,64,16,256]{3,2,0,1:T(8,128)(2,1)}, u32[]{:S(2)}, u32[]{:S(2)}) async-start(bf16[4,64,16,256]{3,2,0,1:T(8,128)(2,1)} %copy.79), calls=%async_computation.3 | async-start | bytes 4194304 | tf_op jit(solution)/shard_map/all_to_all | solution.py:91
  255.8 26.7 %copy-start.11 = (f32[512]{0:T(512)S(1)}, f32[512]{0:T(512)}, u32[]{:S(2)}) copy-start(f32[512]{0:T(512)} %param.30) | copy-start | bytes 6148
where the time goes:
time: 290 us; the launch traced here: 287 us
  waiting for transfers between devices  85.5 us (29%)
  blocking collectives  56.3 us (19%)
  matrix products  55.2 us (19%)
  local copies, waits for them, and re-layouts  52.5 us (18%)
  starting transfers between devices  23.8 us (8%)
  other arithmetic  13.1 us (5%)
    all_to_all x1, waiting for transfers between devices, shards(): lax.all_to_all(lax.all_to_all(per_pin.reshape(groups, members, slot_count...  46.8 us
    dot_general x16, matrix products, add_block(): lax.dot_general(selector, block_values, (((0,), (0,)), ((), ())), preferr...  43.6 us
    all_to_all x1, waiting for transfers between devices, shards(): lax.all_to_all(lax.all_to_all(outgoing, 'grp', split_axis=0, concat_axis=...  38.7 us
    all_to_all x1, blocking collectives, shards(): lax.all_to_all(outgoing, 'grp', split_axis=0, concat_axis=0, tiled=True)  29.9 us
    all_to_all x1, blocking collectives, shards(): lax.all_to_all(per_pin.reshape(groups, members, slot_count, feat_width),...  26.4 us
    gather x1, local copies, waits for them, and re-layouts, shards(): jnp.take(message, net_ids, axis=0)  16.9 us
    gather x1, local copies, waits for them, and re-layouts, shards(): jnp.take(pin_feat, node_picks, axis=0)  14.6 us
    all_to_all x1, starting transfers between devices, shards(): lax.all_to_all(lax.all_to_all(outgoing, 'grp', split_axis=0, concat_axis=...  13.8 us
  transfers between devices with their start and end apart: 2, of which 2 were waited for; matrix products, arithmetic and copies ran while one was open for 5% of the time, Pallas kernels for 0%

commit v1 on v0

v1 whole, which is shorter than its diff:
```python
import functools

import jax
import jax.numpy as jnp
from jax import lax
from jax.experimental import pallas as pl
from jax.experimental.pallas import tpu as pltpu
from jax.sharding import PartitionSpec as P

MESH = pl.DeviceIdType.MESH
BF16 = jnp.bfloat16
F32 = jnp.float32

XS = 4
ZS = 8
QS = 8
SLOTS = 16
PEERS = XS * QS
CHUNK = PEERS * SLOTS
NODES = 2048
NETS = 1024
H = 256
FF = 512


def dot(a, b):
    return jnp.dot(a, b, preferred_element_type=F32)


def chunk_offset(step):
    return 4 + (1 - 2 * lax.rem(step, 2)) * lax.div(step + 1, 2)


def select_rows(table, ids_ref, plane, count):
    picked = []
    for part in range(XS):
        ids = ids_ref[plane, pl.ds(part, 1), :]
        columns = jnp.transpose(jnp.broadcast_to(ids, (128, 128)))
        columns = jnp.concatenate([columns] * (count // 128), axis=1)
        places = lax.broadcasted_iota(jnp.int32, (128, count), 1)
        picked.append(jnp.where(columns == places, 1.0, 0.0).astype(BF16))
    return dot(jnp.concatenate(picked, axis=0), table)


def onehot_t(ids_ref, plane, base, count):
    ids = jnp.concatenate([ids_ref[plane, pl.ds(part, 1), :] for part in range(XS)], axis=1)
    places = lax.broadcasted_iota(jnp.int32, (count, CHUNK), 0) + base
    return jnp.where(ids == places, 1.0, 0.0).astype(BF16)


def layer_kernel(
    x_ref, node_ids, net_ids,
    pin_w1, pin_b1, pin_w2, net_w1, net_b1, net_w2, self_w, msg_w, node_b, out_w,
    o_ref,
    table, out1, in1, out2, in2, net_acc, net_inv, node_acc, self_part,
    send1, recv1, send2, recv2,
):
    x = lax.axis_index("grp")
    dev = lax.axis_index("dev")
    z = lax.div(dev, QS)
    q = lax.rem(dev, QS)

    barrier = pltpu.get_barrier_semaphore()
    for dx in range(XS):
        tx = lax.rem(x + dx, XS)

        @pl.loop(0, ZS)
        def _(dz, tx=tx, dx=dx):
            tz = lax.rem(z + dz, ZS)
            for dq in range(QS):
                target = (tx, tz * QS + lax.rem(q + dq, QS))
                if dx or dq:
                    pl.semaphore_signal(barrier, inc=1, device_id=target, device_id_type=MESH)
                else:
                    @pl.when(dz > 0)
                    def _(target=target):
                        pl.semaphore_signal(barrier, inc=1, device_id=target, device_id_type=MESH)

    @pl.loop(0, NODES // 256)
    def _(tile):
        rows = pl.ds(pl.multiple_of(tile * 256, 256), 256)
        inner = jax.nn.gelu(dot(x_ref[rows, :], pin_w1[...]) + pin_b1[...])
        table[rows, :] = dot(inner.astype(BF16), pin_w2[...]).astype(BF16)

    def send_plane(src, dst, send_sem, recv_sem, tz, first):
        @pl.loop(0, XS)
        def _(dx):
            tx = lax.rem(x + dx, XS)
            for dq in range(QS):
                tq = lax.rem(q + dq, QS)

                def start(tx=tx, tq=tq):
                    pltpu.make_async_remote_copy(
                        src_ref=src.at[tz, tx * QS + tq],
                        dst_ref=dst.at[z, x * QS + q],
                        send_sem=send_sem.at[tz],
                        recv_sem=recv_sem.at[z],
                        device_id=(tx, tz * QS + tq),
                        device_id_type=MESH,
                    ).start()

                if first and dq == 0:
                    pl.when(dx > 0)(start)
                else:
                    start()

        if first:
            pltpu.make_async_copy(src.at[z, x * QS + q], dst.at[z, x * QS + q], recv_sem.at[z]).start()

    def exchange_out(rows_of, src, dst, send_sem, recv_sem, after_first=None):
        def one(step, first=False):
            tz = lax.rem(z + chunk_offset(step), ZS)
            src[tz] = rows_of(tz).astype(BF16).reshape(PEERS, SLOTS, H)
            send_plane(src, dst, send_sem, recv_sem, tz, first)

        src_z = lax.rem(z + 4, ZS)
        src[src_z] = rows_of(src_z).astype(BF16).reshape(PEERS, SLOTS, H)
        if after_first is not None:
            after_first()
        send_plane(src, dst, send_sem, recv_sem, src_z, False)

        @pl.loop(1, ZS - 1)
        def _(step):
            one(step)

        one(ZS - 1, True)

    def wait_in(dst, recv_sem, plane):
        pltpu.make_async_copy(dst.at[plane], dst.at[plane], recv_sem.at[plane]).wait()

    exchange_out(
        lambda tz: select_rows(table[...], node_ids, tz, NODES), out1, in1, send1, recv1,
        lambda: pl.semaphore_wait(barrier, XS * ZS * QS - 1),
    )

    net_acc[...] = jnp.zeros_like(net_acc)
    net_inv[...] = jnp.zeros_like(net_inv)
    ones = jnp.ones((CHUNK, 128), BF16)

    @pl.loop(0, ZS)
    def _(plane):
        net_inv[...] += dot(onehot_t(net_ids, plane, 0, NETS), ones)

    net_inv[...] = 1.0 / net_inv[...]

    @pl.loop(0, NODES // 256)
    def _(tile):
        rows = pl.ds(pl.multiple_of(tile * 256, 256), 256)
        self_part[rows, :] = dot(x_ref[rows, :], self_w[...]) + node_b[...]

    node_acc[...] = jnp.zeros_like(node_acc)

    @pl.loop(0, ZS)
    def _(step):
        sz = lax.rem(z + ZS - chunk_offset(step), ZS)
        wait_in(in1, recv1, sz)
        net_acc[...] += dot(onehot_t(net_ids, sz, 0, NETS), in1[sz].reshape(CHUNK, H))

    @pl.loop(0, NETS // 256)
    def _(tile):
        rows = pl.ds(pl.multiple_of(tile * 256, 256), 256)
        inv = net_inv[rows, :]
        mean = (net_acc[rows, :] * jnp.concatenate([inv, inv], axis=1)).astype(BF16)
        inner = jax.nn.gelu(dot(mean, net_w1[...]) + net_b1[...])
        table[rows, :] = dot(inner.astype(BF16), net_w2[...]).astype(BF16)

    exchange_out(
        lambda tz: select_rows(table[pl.ds(0, NETS), :], net_ids, tz, NETS), out2, in2, send2, recv2,
    )

    @pl.loop(0, ZS)
    def _(step):
        sz = lax.rem(z + ZS - chunk_offset(step), ZS)
        wait_in(in2, recv2, sz)
        rows = in2[sz].reshape(CHUNK, H)
        for half in range(2):
            part = pl.ds(half * NETS, NETS)
            node_acc[part, :] += dot(onehot_t(node_ids, sz, half * NETS, NETS), rows)

    @pl.loop(0, NODES // 256)
    def _(tile):
        rows = pl.ds(pl.multiple_of(tile * 256, 256), 256)
        pre = self_part[rows, :] + dot(node_acc[rows, :].astype(BF16), msg_w[...])
        inner = jax.nn.silu(pre).astype(BF16)
        o_ref[rows, :] = (x_ref[rows, :].astype(F32) + dot(inner, out_w[...])).astype(BF16)

    for src, send_sem in ((out1, send1), (out2, send2)):
        @pl.loop(1, ZS)
        def _(t, src=src, send_sem=send_sem):
            tz = lax.rem(z + t, ZS)
            pltpu.make_async_copy(src.at[tz], src.at[tz], send_sem.at[tz]).wait()

        part = src.at[z, pl.ds(0, PEERS - 1)]
        pltpu.make_async_copy(part, part, send_sem.at[z]).wait()


def layer(x, node_ids, net_ids, *weights):
    dma8 = pltpu.SemaphoreType.DMA((ZS,))
    rows_buf = pltpu.VMEM((ZS, PEERS, SLOTS, H), BF16)
    return pl.pallas_call(
        layer_kernel,
        out_shape=jax.ShapeDtypeStruct((NODES, H), BF16),
        in_specs=[pl.BlockSpec(memory_space=pltpu.VMEM)] * 13,
        out_specs=pl.BlockSpec(memory_space=pltpu.VMEM),
        scratch_shapes=[
            pltpu.VMEM((NODES, H), BF16),
            rows_buf, rows_buf, rows_buf, rows_buf,
            pltpu.VMEM((NETS, H), F32),
            pltpu.VMEM((NETS, 128), F32),
            pltpu.VMEM((NODES, H), F32),
            pltpu.VMEM((NODES, FF), F32),
            dma8, dma8, dma8, dma8,
        ],
        compiler_params=pltpu.CompilerParams(
            collective_id=0, has_side_effects=True, vmem_limit_bytes=56 * 1024 * 1024
        ),
    )(x, node_ids, net_ids, *weights)


def by_plane(ids):
    return ids.reshape(XS, ZS, QS * SLOTS).transpose(1, 0, 2)


def shards(
    node_feat, send_node, pin_net, pin_count,
    pin_w1, pin_b1, pin_w2, net_w1, net_b1, net_w2, self_w, msg_w, node_b, out_w,
):
    slots = lax.broadcasted_iota(jnp.int32, pin_net.shape, 2)
    live_nets = jnp.where(slots < pin_count[:, :, None], pin_net, -1)
    return layer(
        node_feat, by_plane(send_node), by_plane(live_nets),
        pin_w1, pin_b1[None, :], pin_w2, net_w1, net_b1[None, :], net_w2,
        self_w, msg_w, node_b[None, :], out_w,
    )


def solution(mesh):
    owned = ("grp", "dev")
    in_specs = (P(owned, None), P(owned, None, None), P(owned, None, None), P(owned, None)) + (P(),) * 10
    return jax.shard_map(shards, mesh=mesh, in_specs=in_specs, out_specs=P(owned, None), check_vma=False)
```

time: 290 us -> 134 us (0.46)
  Pallas kernels: 0 us -> 128 us
  waiting for transfers between devices: 85.5 us -> 0 us
  blocking collectives: 56.3 us -> 0 us
  matrix products: 55.2 us -> 0 us
  local copies, waits for them, and re-layouts: 52.5 us -> 4.56 us
  starting transfers between devices: 23.8 us -> 0 us
  other arithmetic: 13.1 us -> 0.72 us
    pallas_call x0 -> x1, Pallas kernels: none -> 128 us  [layer(): pl.pallas_call(layer_kernel, out_shape=jax.ShapeDtypeStruct((NODES, H), B...]
    all_to_all x2 -> x0, waiting for transfers between devices: 85.5 us -> none  [the longest x1 46.8 us: shards(): lax.all_to_all(lax.all_to_all(per_pin.reshape(groups, members, slot_count...]
    all_to_all x2 -> x0, blocking collectives: 56.3 us -> none  [the longest x1 29.9 us: shards(): lax.all_to_all(outgoing, 'grp', split_axis=0, concat_axis=0, tiled=True)]
    dot_general x20 -> x0, matrix products: 55.2 us -> none  [the longest x16 43.6 us: add_block(): lax.dot_general(selector, block_values, (((0,), (0,)), ((), ())), preferr...]
    gather x2 -> x0, local copies, waits for them, and re-layouts: 31.6 us -> none  [the longest x1 16.9 us: shards(): jnp.take(message, net_ids, axis=0)]
    all_to_all x2 -> x0, starting transfers between devices: 23.8 us -> none  [the longest x1 13.8 us: shards(): lax.all_to_all(lax.all_to_all(outgoing, 'grp', split_axis=0, concat_axis=...]
    all_to_all x4 -> x0, local copies, waits for them, and re-layouts: 7.95 us -> none  [the longest x1 3.13 us: shards(): lax.all_to_all(lax.all_to_all(per_pin.reshape(groups, members, slot_count...]
    select_n x5 -> x1, other arithmetic: 7.27 us -> 0.72 us  [shards(): live_nets = jnp.where(slots < pin_count[:, :, None], pin_net, -1)]
  transfers between devices with their start and end apart: 2 -> 0, of which waited for: 2 -> 0; matrix products, arithmetic and copies ran while one was open for 5% -> 0% of each run, Pallas kernels for 0% -> 0%
where the time goes in v1:
time: 134 us; the launch traced here: 133 us
  Pallas kernels  128 us (96%)
  local copies, waits for them, and re-layouts  4.56 us (3%)
    pallas_call x1, Pallas kernels, layer(): pl.pallas_call(layer_kernel, out_shape=jax.ShapeDtypeStruct((NODES, H), B...  128 us
    unnamed x6, local copies, waits for them, and re-layouts  3.65 us

profile of v1, /device:TPU:1, one launch (start us, length us, event | category | flops | bytes accessed | tf_op | source)
XLA Modules:
  0.0 133.5 jit_solution(6306224016791409354)
XLA Ops:
  0.0 0.0 copy-start.1
  0.0 0.7 copy-done.1
  0.7 0.7 fusion
  1.4 0.1 copy.17
  1.5 0.0 copy-start
  1.5 0.1 reshape.42
  1.6 0.6 copy-done
  2.2 0.1 copy.15
  2.3 0.1 reshape.41
  2.4 0.6 copy_bitcast_fusion
  3.0 128.2 %shard_map.139 = bf16[2048,256]{1,0:T(8,128)(2,1)} custom-call(bf16[2048,256]{1,0:T(8,128)(2,1)} %x_ref.1, s32[8,4,128]{2,1,0:T(4,128)} %get-tuple-element.6.node_ids, s32[8,4,128]{2,1,0:T(4,128)} %get-tuple-element.5.net_ids, bf16[256,512]{1,0:T(8,128)(2,1)} %pin_w1.1, f32[1,512]{1,0:T(1,128)} %bitcast.8, bf16[512,256]{1,0:T(8,128)(2,1)} %pin_w2.1, ...), custom_call_target="tpu_custom_call" | custom-call | tf_op jit(solution)/shard_map/pallas_call | solution.py:200
  131.2 2.3 %copy.22 = bf16[2048,256]{1,0:T(8,128)(2,1)} copy(bf16[2048,256]{1,0:T(8,128)(2,1)} %shard_map.139) | data formatting | bytes 2097152
Async XLA Ops:
  0.0 0.7 copy-start.1
  1.5 0.7 copy-start

commit v2 on v1

v2 whole, which is shorter than its diff:
```python
import jax
import jax.numpy as jnp
from jax import lax
from jax.experimental import pallas as pl
from jax.experimental.pallas import tpu as pltpu
from jax.sharding import PartitionSpec as P

MESH = pl.DeviceIdType.MESH
BF16 = jnp.bfloat16
F32 = jnp.float32

XS = 4
ZS = 8
QS = 8
SLOTS = 16
PEERS = XS * ZS
CHUNK = PEERS * SLOTS
OWNERS = XS * ZS * QS
NODES = 2048
NETS = 1024
H = 256
FF = 512
TILE = 256
OPERANDS = 14


def dot(a, b):
    return jnp.dot(a, b, preferred_element_type=F32)


def dot_nt(a, b):
    return lax.dot_general(a, b, (((1,), (1,)), ((), ())), preferred_element_type=F32)


def offset(step):
    return 4 + (1 - 2 * lax.rem(step, 2)) * lax.div(step + 1, 2)


def iota(shape, axis):
    return lax.broadcasted_iota(jnp.int32, shape, axis)


def split_ids(ids):
    high = lax.shift_right_logical(ids, 8)
    low = lax.bitwise_and(ids, 255)
    return jnp.concatenate([high, low], axis=0).astype(F32).astype(BF16)


def chunk_digits(digits, q):
    pin = iota((CHUNK, OWNERS), 0)
    owner = lax.div(pin, ZS * SLOTS) * (ZS * QS) + lax.rem(lax.div(pin, SLOTS), ZS) * QS
    take = jnp.where(iota((CHUNK, OWNERS), 1) - q == owner, 1.0, 0.0).astype(BF16)
    spread = dot_nt(take, digits)
    own_slot = lax.rem(iota((CHUNK, 2 * SLOTS), 1), SLOTS) == lax.rem(iota((CHUNK, 2 * SLOTS), 0), SLOTS)
    return jnp.where(own_slot, spread, 0.0).astype(BF16)


def ids_down(digits, q):
    weights = jnp.where(iota((2 * SLOTS, 128), 0) < SLOTS, 256.0, 1.0).astype(BF16)
    return dot(chunk_digits(digits, q), weights).astype(jnp.int32)


def ids_across(digits, q):
    weights = jnp.where(iota((8, 2 * SLOTS), 1) < SLOTS, 256.0, 1.0).astype(BF16)
    return dot_nt(weights, chunk_digits(digits, q))[0:1, :].astype(jnp.int32)


def select_rows(table, digits, q, count):
    ids = jnp.concatenate([ids_down(digits, q)] * (count // 128), axis=1)
    picked = jnp.where(ids == iota((CHUNK, count), 1), 1.0, 0.0).astype(BF16)
    return dot(picked, table).astype(BF16).reshape(PEERS, SLOTS, H)


def members(ids, base, count):
    return jnp.where(ids == iota((count, CHUNK), 0) + base, 1.0, 0.0).astype(BF16)


def layer_kernel(*refs):
    hbm, o_ref, vmem = refs[:OPERANDS], refs[OPERANDS], refs[OPERANDS + 1 : 2 * OPERANDS + 1]
    (
        table, out1, in1, out2, in2, net_acc, net_inv, node_acc, self_part, node_digits, net_digits,
        load, send1, recv1, send2, recv2, column_sem,
    ) = refs[2 * OPERANDS + 1 :]
    (
        node_ids, x_ref, pin_w1, pin_b1, pin_w2, net_ids, counts,
        net_w1, net_b1, net_w2, self_w, msg_w, node_b, out_w,
    ) = vmem
    x = lax.axis_index("grp")
    dev = lax.axis_index("dev")
    z = lax.div(dev, QS)
    q = lax.rem(dev, QS)
    place = x * ZS + z

    loads = [pltpu.make_async_copy(a, b, load.at[i]) for i, (a, b) in enumerate(zip(hbm, vmem))]
    for copy in loads:
        copy.start()

    def signal(sem, dx, dz, dq):
        target = (lax.rem(x + dx, XS), lax.rem(z + dz, ZS) * QS + lax.rem(q + dq, QS))
        pl.semaphore_signal(sem, inc=1, device_id=target, device_id_type=MESH)

    barrier = pltpu.get_barrier_semaphore()
    for dz in (4, 3, 5, 2, 6, 1, 7):
        signal(barrier, 0, dz, 0)
    for dx in range(XS):
        for dq in range(QS):
            if dx or dq:
                signal(barrier, dx, 0, dq)

    def rows_of(tile):
        return pl.ds(pl.multiple_of(tile * TILE, TILE), TILE)

    def transform(tile):
        rows = rows_of(tile)
        inner = jax.nn.gelu(dot(x_ref[rows, :], pin_w1[...]) + pin_b1[...])
        table[rows, :] = dot(inner.astype(BF16), pin_w2[...]).astype(BF16)

    for copy in loads[:5]:
        copy.wait()
    node_digits[...] = split_ids(node_ids[...])
    pl.loop(0, 6)(transform)
    pl.semaphore_wait(barrier, XS * QS - 1 + ZS - 1)
    for dz in (4, 3, 5, 2, 6, 1, 7):
        signal(column_sem, 0, dz, 0)
    pl.loop(6, NODES // TILE)(transform)

    def send_chunk(src, dst, send_sem, recv_sem, tq, own):
        for dz in (4, 3, 5, 2, 6, 1, 7, 0):
            tz = lax.rem(z + dz, ZS)
            for dx in range(XS):
                tx = lax.rem(x + dx, XS)
                if own and dz == 0 and dx == 0:
                    pltpu.make_async_copy(src.at[q, place], dst.at[q, place], recv_sem.at[q]).start()
                else:
                    pltpu.make_async_remote_copy(
                        src_ref=src.at[tq, tx * ZS + tz],
                        dst_ref=dst.at[q, place],
                        send_sem=send_sem.at[tq],
                        recv_sem=recv_sem.at[q],
                        device_id=(tx, tz * QS + tq),
                        device_id_type=MESH,
                    ).start()

    def exchange_out(rows_for, src, dst, send_sem, recv_sem, before_send=None):
        first_q = lax.rem(q + 4, QS)
        src[first_q] = rows_for(first_q)
        if before_send is not None:
            before_send()
        send_chunk(src, dst, send_sem, recv_sem, first_q, False)

        @pl.loop(1, QS - 1)
        def _(step):
            tq = lax.rem(q + offset(step), QS)
            src[tq] = rows_for(tq)
            send_chunk(src, dst, send_sem, recv_sem, tq, False)

        src[q] = rows_for(q)
        send_chunk(src, dst, send_sem, recv_sem, q, True)

    exchange_out(
        lambda tq: select_rows(table[...], node_digits[...], tq, NODES), out1, in1, send1, recv1,
        lambda: pl.semaphore_wait(column_sem, ZS - 1),
    )

    for copy in loads[5:]:
        copy.wait()
    live = iota((SLOTS, OWNERS), 0) < counts[...]
    net_digits[...] = split_ids(jnp.where(live, net_ids[...], 4095))
    net_acc[...] = jnp.zeros_like(net_acc)
    net_inv[...] = jnp.zeros_like(net_inv)
    node_acc[...] = jnp.zeros_like(node_acc)
    ones = jnp.ones((CHUNK, 128), BF16)

    @pl.loop(0, QS)
    def _(part):
        net_inv[...] += dot(members(ids_across(net_digits[...], part), 0, NETS), ones)

    net_inv[...] = 1.0 / net_inv[...]

    @pl.loop(0, NODES // TILE)
    def _(tile):
        rows = rows_of(tile)
        self_part[rows, :] = dot(x_ref[rows, :], self_w[...]) + node_b[...]

    def wait_in(dst, recv_sem, part):
        pltpu.make_async_copy(dst.at[part], dst.at[part], recv_sem.at[part]).wait()

    @pl.loop(0, QS)
    def _(step):
        sq = lax.rem(q + QS - offset(step), QS)
        picked = members(ids_across(net_digits[...], sq), 0, NETS)
        wait_in(in1, recv1, sq)
        net_acc[...] += dot(picked, in1[sq].reshape(CHUNK, H))

    @pl.loop(0, NETS // TILE)
    def _(tile):
        rows = rows_of(tile)
        inv = net_inv[rows, :]
        mean = (net_acc[rows, :] * jnp.concatenate([inv, inv], axis=1)).astype(BF16)
        inner = jax.nn.gelu(dot(mean, net_w1[...]) + net_b1[...])
        table[rows, :] = dot(inner.astype(BF16), net_w2[...]).astype(BF16)

    exchange_out(
        lambda tq: select_rows(table[pl.ds(0, NETS), :], net_digits[...], tq, NETS), out2, in2, send2, recv2,
    )

    @pl.loop(0, QS)
    def _(step):
        sq = lax.rem(q + QS - offset(step), QS)
        ids = ids_across(node_digits[...], sq)
        wait_in(in2, recv2, sq)
        rows = in2[sq].reshape(CHUNK, H)
        for half in range(2):
            part = pl.ds(half * NETS, NETS)
            node_acc[part, :] += dot(members(ids, half * NETS, NETS), rows)

    @pl.loop(0, NODES // TILE)
    def _(tile):
        rows = rows_of(tile)
        pre = self_part[rows, :] + dot(node_acc[rows, :].astype(BF16), msg_w[...])
        inner = jax.nn.silu(pre).astype(BF16)
        o_ref[rows, :] = (x_ref[rows, :].astype(F32) + dot(inner, out_w[...])).astype(BF16)

    for src, send_sem in ((out1, send1), (out2, send2)):
        @pl.loop(1, QS)
        def _(t, src=src, send_sem=send_sem):
            tq = lax.rem(q + t, QS)
            pltpu.make_async_copy(src.at[tq], src.at[tq], send_sem.at[tq]).wait()

        sent = src.at[q, pl.ds(0, PEERS - 1)]
        pltpu.make_async_copy(sent, sent, send_sem.at[q]).wait()


def layer(*operands):
    loads = pltpu.SemaphoreType.DMA((OPERANDS,))
    eight = pltpu.SemaphoreType.DMA((QS,))
    rows_buf = pltpu.VMEM((QS, PEERS, SLOTS, H), BF16)
    digits = pltpu.VMEM((2 * SLOTS, OWNERS), BF16)
    return pl.pallas_call(
        layer_kernel,
        out_shape=jax.ShapeDtypeStruct((NODES, H), BF16),
        in_specs=[pl.BlockSpec(memory_space=pltpu.HBM)] * OPERANDS,
        out_specs=pl.BlockSpec(memory_space=pltpu.VMEM),
        scratch_shapes=[pltpu.VMEM(a.shape, a.dtype) for a in operands]
        + [
            pltpu.VMEM((NODES, H), BF16),
            rows_buf, rows_buf, rows_buf, rows_buf,
            pltpu.VMEM((NETS, H), F32),
            pltpu.VMEM((NETS, 128), F32),
            pltpu.VMEM((NODES, H), F32),
            pltpu.VMEM((NODES, FF), F32),
            digits, digits,
            loads, eight, eight, eight, eight,
            pltpu.SemaphoreType.REGULAR,
        ],
        compiler_params=pltpu.CompilerParams(
            collective_id=0, has_side_effects=True, vmem_limit_bytes=56 * 1024 * 1024
        ),
    )(*operands)


def shards(
    node_feat, send_node, pin_net, pin_count,
    pin_w1, pin_b1, pin_w2, net_w1, net_b1, net_w2, self_w, msg_w, node_b, out_w,
):
    return layer(
        send_node[0].T, node_feat, pin_w1, pin_b1[None, :], pin_w2, pin_net[0].T, pin_count,
        net_w1, net_b1[None, :], net_w2, self_w, msg_w, node_b[None, :], out_w,
    )


def solution(mesh):
    owned = ("grp", "dev")
    in_specs = (P(owned, None), P(owned, None, None), P(owned, None, None), P(owned, None)) + (P(),) * 10
    return jax.shard_map(shards, mesh=mesh, in_specs=in_specs, out_specs=P(owned, None), check_vma=False)
```

time: 134 us -> 120 us (0.90)
  Pallas kernels: 128 us -> 117 us
  local copies, waits for them, and re-layouts: 4.56 us -> 2.26 us
    pallas_call x1, Pallas kernels: 128 us -> 117 us  [layer(): pl.pallas_call(layer_kernel, out_shape=jax.ShapeDtypeStruct((NODES, H), B...]
    unnamed x6 -> x1, local copies, waits for them, and re-layouts: 3.65 us -> 2.26 us
where the time goes in v2:
time: 120 us
  Pallas kernels  117 us (98%)
  local copies, waits for them, and re-layouts  2.26 us (2%)
    pallas_call x1, Pallas kernels, layer(): pl.pallas_call(layer_kernel, out_shape=jax.ShapeDtypeStruct((NODES, H), B...  117 us

profile of v2, /device:TPU:1, one launch (start us, length us, event | category | flops | bytes accessed | tf_op | source)
XLA Modules:
  0.0 119.8 jit_solution(17759432908568401968)
XLA Ops:
  0.0 117.5 %shard_map.136 = bf16[2048,256]{1,0:T(8,128)(2,1)} custom-call(s32[16,256]{1,0:T(8,128)} %bitcast.9, bf16[2048,256]{1,0:T(8,128)(2,1)} %refs_1_.1, bf16[256,512]{1,0:T(8,128)(2,1)} %refs_2_.1, f32[1,512]{1,0:T(1,128)} %bitcast.11, bf16[512,256]{1,0:T(8,128)(2,1)} %refs_4_.1, s32[16,256]{1,0:T(8,128)} %bitcast.10, s32[1,256]{1,0:T(1,128)} %refs_6_.1, ...), custom_call_target="tpu_custom_call" | custom-call | tf_op jit(solution)/shard_map/pallas_call | solution.py:239
  117.5 2.3 %copy.16 = bf16[2048,256]{1,0:T(8,128)(2,1)} copy(bf16[2048,256]{1,0:T(8,128)(2,1)} %shard_map.136) | data formatting | bytes 2097152

commit v3 on v2

v3 whole, which is shorter than its diff:
```python
import jax
import jax.numpy as jnp
from jax import lax
from jax.experimental import pallas as pl
from jax.experimental.pallas import tpu as pltpu
from jax.sharding import PartitionSpec as P

MESH = pl.DeviceIdType.MESH
BF16 = jnp.bfloat16
F32 = jnp.float32

XS = 4
ZS = 8
QS = 8
SLOTS = 16
PEERS = XS * QS
CHUNK = PEERS * SLOTS
OWNERS = XS * ZS * QS
NODES = 2048
NETS = 1024
H = 256
FF = 512
TILE = 256
OPERANDS = 14


def dot(a, b):
    return jnp.dot(a, b, preferred_element_type=F32)


def dot_nt(a, b):
    return lax.dot_general(a, b, (((1,), (1,)), ((), ())), preferred_element_type=F32)


def iota(shape, axis):
    return lax.broadcasted_iota(jnp.int32, shape, axis)


def split_ids(ids):
    high = lax.shift_right_logical(ids, 8)
    low = lax.bitwise_and(ids, 255)
    return jnp.concatenate([high, low], axis=0).astype(F32).astype(BF16)


def chunk_digits(digits, plane):
    pin = iota((CHUNK, OWNERS), 0)
    owner = lax.div(pin, QS * SLOTS) * (ZS * QS) + lax.rem(lax.div(pin, SLOTS), QS)
    take = jnp.where(iota((CHUNK, OWNERS), 1) - plane * QS == owner, 1.0, 0.0).astype(BF16)
    spread = dot_nt(take, digits)
    own_slot = lax.rem(iota((CHUNK, 2 * SLOTS), 1), SLOTS) == lax.rem(iota((CHUNK, 2 * SLOTS), 0), SLOTS)
    return jnp.where(own_slot, spread, 0.0).astype(BF16)


def ids_down(digits, plane):
    weights = jnp.where(iota((2 * SLOTS, 128), 0) < SLOTS, 256.0, 1.0).astype(BF16)
    return dot(chunk_digits(digits, plane), weights).astype(jnp.int32)


def ids_across(digits, plane):
    weights = jnp.where(iota((8, 2 * SLOTS), 1) < SLOTS, 256.0, 1.0).astype(BF16)
    return dot_nt(weights, chunk_digits(digits, plane))[0:1, :].astype(jnp.int32)


def select_rows(table, digits, plane, count):
    ids = jnp.concatenate([ids_down(digits, plane)] * (count // 128), axis=1)
    picked = jnp.where(ids == iota((CHUNK, count), 1), 1.0, 0.0).astype(BF16)
    return dot(picked, table).astype(BF16).reshape(PEERS, SLOTS, H)


def members(ids, base, count):
    return jnp.where(ids == iota((count, CHUNK), 0) + base, 1.0, 0.0).astype(BF16)


def layer_kernel(*refs):
    hbm, o_ref, vmem = refs[:OPERANDS], refs[OPERANDS], refs[OPERANDS + 1 : 2 * OPERANDS + 1]
    (
        table, out1, in1, out2, in2, sums_out, sums_in, messages_in, ids_out, ids_in,
        net_acc, up_acc, down_acc, net_inv, node_acc, self_part, node_digits, net_digits, up_digits, down_digits,
        load, send1, recv1, send2, recv2, send_sums, recv_sums, send_messages, recv_messages, send_ids, recv_ids, column_sem,
    ) = refs[2 * OPERANDS + 1 :]
    (
        node_ids, net_ids, counts, x_ref, pin_w1, pin_b1, pin_w2,
        net_w1, net_b1, net_w2, self_w, msg_w, node_b, out_w,
    ) = vmem
    x = lax.axis_index("grp")
    dev = lax.axis_index("dev")
    z = lax.div(dev, QS)
    q = lax.rem(dev, QS)
    place = x * QS + q

    def plane(dz):
        return lax.rem(z + dz + 2 * ZS, ZS)

    up = (x, plane(1) * QS + q)
    down = (x, plane(-1) * QS + q)

    loads = [pltpu.make_async_copy(a, b, load.at[i]) for i, (a, b) in enumerate(zip(hbm, vmem))]
    for copy in loads:
        copy.start()

    def signal(sem, dx, dz, dq):
        target = (lax.rem(x + dx, XS), plane(dz) * QS + lax.rem(q + dq, QS))
        pl.semaphore_signal(sem, inc=1, device_id=target, device_id_type=MESH)

    barrier = pltpu.get_barrier_semaphore()
    for dz in (4, 3, 5, 2, 6, 1, 7):
        signal(barrier, 0, dz, 0)
    for dx in range(XS):
        for dq in range(QS):
            if dx or dq:
                signal(barrier, dx, 0, dq)

    def rows_of(tile):
        return pl.ds(pl.multiple_of(tile * TILE, TILE), TILE)

    def transform(tile):
        rows = rows_of(tile)
        inner = jax.nn.gelu(dot(x_ref[rows, :], pin_w1[...]) + pin_b1[...])
        table[rows, :] = dot(inner.astype(BF16), pin_w2[...]).astype(BF16)

    for copy in loads[:7]:
        copy.wait()
    node_digits[...] = split_ids(node_ids[...])
    live_ids = jnp.where(iota((SLOTS, OWNERS), 0) < counts[...], net_ids[...], 4095)
    ids_out[...] = live_ids
    net_digits[...] = split_ids(live_ids)
    pl.loop(0, 6)(transform)
    pl.semaphore_wait(barrier, XS * QS - 1 + ZS - 1)
    for dz in (4, 3, 5, 2, 6, 1, 7):
        signal(column_sem, 0, dz, 0)
    pl.loop(6, NODES // TILE)(transform)

    def remote(src, dst, send_sem, recv_sem, device):
        return pltpu.make_async_remote_copy(
            src_ref=src, dst_ref=dst, send_sem=send_sem, recv_sem=recv_sem, device_id=device, device_id_type=MESH
        )

    def send_chunk(src, dst, send_sem, recv_sem, kind, tz, own):
        for dq in range(QS):
            tq = lax.rem(q + dq, QS)
            for dx in range(XS):
                tx = lax.rem(x + dx, XS)
                copy = remote(
                    src.at[kind, tx * QS + tq], dst.at[kind, place], send_sem.at[kind], recv_sem.at[kind], (tx, tz * QS + tq)
                )
                if dx or dq:
                    copy.start()
                else:
                    pl.when(jnp.logical_not(own))(copy.start)
                    pl.when(own)(pltpu.make_async_copy(src.at[kind, place], dst.at[kind, place], recv_sem.at[kind]).start)

    def wait_in(dst, recv_sem, kind):
        pltpu.make_async_copy(dst.at[kind], dst.at[kind], recv_sem.at[kind]).wait()

    def gather_nodes(kind):
        out1[kind] = select_rows(table[...], node_digits[...], plane(kind), NODES)

    @pl.loop(0, 3)
    def _(j):
        far = 3 - j
        gather_nodes(far)

        @pl.when(j == 0)
        def _():
            pl.semaphore_wait(column_sem, ZS - 1)

        send_chunk(out1, in1, send1, recv1, far, plane(far - 1), j == 2)
        gather_nodes(ZS - far)
        send_chunk(out1, in1, send1, recv1, ZS - far, plane(1 - far), j == 2)

    id_copies = (
        remote(ids_out, ids_in.at[0], send_ids.at[0], recv_ids.at[0], up),
        remote(ids_out, ids_in.at[1], send_ids.at[1], recv_ids.at[1], down),
    )
    for copy in id_copies:
        copy.start()

    @pl.loop(0, 2)
    def _(j):
        kind = 4 - 4 * j
        gather_nodes(kind)
        send_chunk(out1, in1, send1, recv1, kind, plane(kind), j == 1)

    up_acc[...] = jnp.zeros_like(up_acc)
    down_acc[...] = jnp.zeros_like(down_acc)
    net_acc[...] = jnp.zeros_like(net_acc)
    net_inv[...] = jnp.zeros_like(net_inv)
    ones = jnp.ones((CHUNK, 128), BF16)

    @pl.loop(0, ZS)
    def _(part):
        net_inv[...] += dot(members(ids_across(net_digits[...], part), 0, NETS), ones)

    net_inv[...] = 1.0 / net_inv[...]
    for copy in id_copies:
        copy.wait_recv()
    down_digits[...] = split_ids(ids_in[0])
    up_digits[...] = split_ids(ids_in[1])

    def add_nets(acc, digits, kind, from_plane):
        picked = members(ids_across(digits[...], from_plane), 0, NETS)
        wait_in(in1, recv1, kind)
        acc[...] += dot(picked, in1[kind].reshape(CHUNK, H))

    @pl.loop(0, 3)
    def _(j):
        far = 3 - j
        add_nets(up_acc, up_digits, far, plane(1 - far))
        add_nets(down_acc, down_digits, ZS - far, plane(far - 1))

    sums_out[0] = up_acc[...].astype(BF16)
    sums_out[1] = down_acc[...].astype(BF16)
    sum_copies = (
        remote(sums_out.at[0], sums_in.at[0], send_sums.at[0], recv_sums.at[0], up),
        remote(sums_out.at[1], sums_in.at[1], send_sums.at[1], recv_sums.at[1], down),
    )
    for copy in sum_copies:
        copy.start()

    for copy in loads[7:]:
        copy.wait()
    node_acc[...] = jnp.zeros_like(node_acc)

    @pl.loop(0, NODES // TILE)
    def _(tile):
        rows = rows_of(tile)
        self_part[rows, :] = dot(x_ref[rows, :], self_w[...]) + node_b[...]

    @pl.loop(0, 2)
    def _(j):
        kind = 4 * j
        add_nets(net_acc, net_digits, kind, plane(-kind))

    for copy in sum_copies:
        copy.wait_recv()

    def message_copies(rows):
        return (
            remote(table.at[rows, :], messages_in.at[0, rows, :], send_messages.at[0], recv_messages.at[0], up),
            remote(table.at[rows, :], messages_in.at[1, rows, :], send_messages.at[1], recv_messages.at[1], down),
        )

    @pl.loop(0, NETS // TILE)
    def _(tile):
        rows = rows_of(tile)
        inv = net_inv[rows, :]
        total = net_acc[rows, :] + sums_in[0, rows, :].astype(F32) + sums_in[1, rows, :].astype(F32)
        mean = (total * jnp.concatenate([inv, inv], axis=1)).astype(BF16)
        inner = jax.nn.gelu(dot(mean, net_w1[...]) + net_b1[...])
        table[rows, :] = dot(inner.astype(BF16), net_w2[...]).astype(BF16)
        for copy in message_copies(rows):
            copy.start()

    @pl.loop(0, 2)
    def _(j):
        kind = 4 - 4 * j
        out2[kind] = select_rows(table[pl.ds(0, NETS), :], net_digits[...], plane(kind), NETS)
        send_chunk(out2, in2, send2, recv2, kind, plane(kind), j == 1)

    for copy in message_copies(pl.ds(0, NETS)):
        copy.wait_recv()

    @pl.loop(0, 3)
    def _(j):
        far = 3 - j
        out2[far] = select_rows(messages_in[1], up_digits[...], plane(1 - far), NETS)
        send_chunk(out2, in2, send2, recv2, far, plane(1 - far), j == 2)
        out2[ZS - far] = select_rows(messages_in[0], down_digits[...], plane(far - 1), NETS)
        send_chunk(out2, in2, send2, recv2, ZS - far, plane(far - 1), j == 2)

    def add_nodes(kind):
        ids = ids_across(node_digits[...], plane(kind))
        wait_in(in2, recv2, kind)
        rows = in2[kind].reshape(CHUNK, H)
        for half in range(2):
            part = pl.ds(half * NETS, NETS)
            node_acc[part, :] += dot(members(ids, half * NETS, NETS), rows)

    @pl.loop(0, 2)
    def _(j):
        add_nodes(4 * j)

    @pl.loop(0, 3)
    def _(j):
        add_nodes(3 - j)
        add_nodes(5 + j)

    @pl.loop(0, NODES // TILE)
    def _(tile):
        rows = rows_of(tile)
        pre = self_part[rows, :] + dot(node_acc[rows, :].astype(BF16), msg_w[...])
        inner = jax.nn.silu(pre).astype(BF16)
        o_ref[rows, :] = (x_ref[rows, :].astype(F32) + dot(inner, out_w[...])).astype(BF16)

    for src, send_sem in ((out1, send1), (out2, send2)):
        for kind in range(ZS):
            sent = src.at[kind, pl.ds(0, PEERS - 1)] if kind in (0, 1, 7) else src.at[kind]
            pltpu.make_async_copy(sent, sent, send_sem.at[kind]).wait()
    for copy in id_copies + sum_copies + message_copies(pl.ds(0, NETS)):
        copy.wait_send()


def layer(*operands):
    loads = pltpu.SemaphoreType.DMA((OPERANDS,))
    eight = pltpu.SemaphoreType.DMA((ZS,))
    pair = pltpu.SemaphoreType.DMA((2,))
    rows_buf = pltpu.VMEM((ZS, PEERS, SLOTS, H), BF16)
    net_rows = pltpu.VMEM((2, NETS, H), BF16)
    net_sums = pltpu.VMEM((NETS, H), F32)
    digits = pltpu.VMEM((2 * SLOTS, OWNERS), BF16)
    return pl.pallas_call(
        layer_kernel,
        out_shape=jax.ShapeDtypeStruct((NODES, H), BF16),
        in_specs=[pl.BlockSpec(memory_space=pltpu.HBM)] * OPERANDS,
        out_specs=pl.BlockSpec(memory_space=pltpu.VMEM),
        scratch_shapes=[pltpu.VMEM(a.shape, a.dtype) for a in operands]
        + [
            pltpu.VMEM((NODES, H), BF16),
            rows_buf, rows_buf, rows_buf, rows_buf,
            net_rows, net_rows, net_rows,
            pltpu.VMEM((SLOTS, OWNERS), jnp.int32),
            pltpu.VMEM((2, SLOTS, OWNERS), jnp.int32),
            net_sums, net_sums, net_sums,
            pltpu.VMEM((NETS, 128), F32),
            pltpu.VMEM((NODES, H), F32),
            pltpu.VMEM((NODES, FF), F32),
            digits, digits, digits, digits,
            loads, eight, eight, eight, eight, pair, pair, pair, pair, pair, pair,
            pltpu.SemaphoreType.REGULAR,
        ],
        compiler_params=pltpu.CompilerParams(
            collective_id=0, has_side_effects=True, vmem_limit_bytes=56 * 1024 * 1024
        ),
    )(*operands)


def shards(
    node_feat, send_node, pin_net, pin_count,
    pin_w1, pin_b1, pin_w2, net_w1, net_b1, net_w2, self_w, msg_w, node_b, out_w,
):
    return layer(
        send_node[0].T, pin_net[0].T, pin_count, node_feat, pin_w1, pin_b1[None, :], pin_w2,
        net_w1, net_b1[None, :], net_w2, self_w, msg_w, node_b[None, :], out_w,
    )


def solution(mesh):
    owned = ("grp", "dev")
    in_specs = (P(owned, None), P(owned, None, None), P(owned, None, None), P(owned, None)) + (P(),) * 10
    return jax.shard_map(shards, mesh=mesh, in_specs=in_specs, out_specs=P(owned, None), check_vma=False)
```

time: 120 us -> 114 us (0.950)
  Pallas kernels: 117 us -> 112 us
    pallas_call x1, Pallas kernels: 117 us -> 112 us  [layer(): pl.pallas_call(layer_kernel, out_shape=jax.ShapeDtypeStruct((NODES, H), B...]
where the time goes in v3:
time: 114 us
  Pallas kernels  112 us (98%)
  local copies, waits for them, and re-layouts  2.26 us (2%)
    pallas_call x1, Pallas kernels, layer(): pl.pallas_call(layer_kernel, out_shape=jax.ShapeDtypeStruct((NODES, H), B...  112 us

profile of v3, /device:TPU:1, one launch (start us, length us, event | category | flops | bytes accessed | tf_op | source)
XLA Modules:
  0.0 114.1 jit_solution(13809808233835717612)
XLA Ops:
  0.0 111.9 %shard_map.136 = bf16[2048,256]{1,0:T(8,128)(2,1)} custom-call(s32[16,256]{1,0:T(8,128)} %bitcast.9, s32[16,256]{1,0:T(8,128)} %bitcast.10, s32[1,256]{1,0:T(1,128)} %refs_2_.1, bf16[2048,256]{1,0:T(8,128)(2,1)} %refs_3_.1, bf16[256,512]{1,0:T(8,128)(2,1)} %refs_4_.1, f32[1,512]{1,0:T(1,128)} %bitcast.11, bf16[512,256]{1,0:T(8,128)(2,1)} %refs_6_.1, ...), custom_call_target="tpu_custom_call" | custom-call | tf_op jit(solution)/shard_map/pallas_call | solution.py:311
  111.9 2.3 %copy.16 = bf16[2048,256]{1,0:T(8,128)(2,1)} copy(bf16[2048,256]{1,0:T(8,128)(2,1)} %shard_map.136) | data formatting | bytes 2097152

commit v4 on v3

--- a/solution.py
+++ b/solution.py
@@ -136,10 +136,10 @@
         )
 
     def send_chunk(src, dst, send_sem, recv_sem, kind, tz, own):
-        for dq in range(QS):
-            tq = lax.rem(q + dq, QS)
-            for dx in range(XS):
-                tx = lax.rem(x + dx, XS)
+        for dx in (2, 1, 3, 0):
+            tx = lax.rem(x + dx, XS)
+            for dq in (4, 3, 5, 2, 6, 1, 7, 0):
+                tq = lax.rem(q + dq, QS)
                 copy = remote(
                     src.at[kind, tx * QS + tq], dst.at[kind, place], send_sem.at[kind], recv_sem.at[kind], (tx, tz * QS + tq)
                 )
@@ -289,7 +289,7 @@
     def _(tile):
         rows = rows_of(tile)
         pre = self_part[rows, :] + dot(node_acc[rows, :].astype(BF16), msg_w[...])
-        inner = jax.nn.silu(pre).astype(BF16)
+        inner = (0.5 * pre * (1.0 + jnp.tanh(0.5 * pre))).astype(BF16)
         o_ref[rows, :] = (x_ref[rows, :].astype(F32) + dot(inner, out_w[...])).astype(BF16)
 
     for src, send_sem in ((out1, send1), (out2, send2)):

time: 114 us -> 114 us (level)
  no operation moved by 1% of the time
where the time goes in v4:
time: 114 us
  Pallas kernels  111 us (97%)
  local copies, waits for them, and re-layouts  2.26 us (2%)
    pallas_call x1, Pallas kernels, layer(): pl.pallas_call(layer_kernel, out_shape=jax.ShapeDtypeStruct((NODES, H), B...  111 us

profile of v4, /device:TPU:1, one launch (start us, length us, event | category | flops | bytes accessed | tf_op | source)
XLA Modules:
  0.0 113.7 jit_solution(5840259050017112316)
XLA Ops:
  0.0 111.4 %shard_map.136 = bf16[2048,256]{1,0:T(8,128)(2,1)} custom-call(s32[16,256]{1,0:T(8,128)} %bitcast.9, s32[16,256]{1,0:T(8,128)} %bitcast.10, s32[1,256]{1,0:T(1,128)} %refs_2_.1, bf16[2048,256]{1,0:T(8,128)(2,1)} %refs_3_.1, bf16[256,512]{1,0:T(8,128)(2,1)} %refs_4_.1, f32[1,512]{1,0:T(1,128)} %bitcast.11, bf16[512,256]{1,0:T(8,128)(2,1)} %refs_6_.1, ...), custom_call_target="tpu_custom_call" | custom-call | tf_op jit(solution)/shard_map/pallas_call | solution.py:311
  111.5 2.3 %copy.16 = bf16[2048,256]{1,0:T(8,128)(2,1)} copy(bf16[2048,256]{1,0:T(8,128)(2,1)} %shard_map.136) | data formatting | bytes 2097152

commit v5 on v4

--- a/solution.py
+++ b/solution.py
@@ -95,7 +95,7 @@
     down = (x, plane(-1) * QS + q)
 
     loads = [pltpu.make_async_copy(a, b, load.at[i]) for i, (a, b) in enumerate(zip(hbm, vmem))]
-    for copy in loads:
+    for copy in loads[:7]:
         copy.start()
 
     def signal(sem, dx, dz, dq):
@@ -129,6 +129,8 @@
     for dz in (4, 3, 5, 2, 6, 1, 7):
         signal(column_sem, 0, dz, 0)
     pl.loop(6, NODES // TILE)(transform)
+    for copy in loads[7:]:
+        copy.start()
 
     def remote(src, dst, send_sem, recv_sem, device):
         return pltpu.make_async_remote_copy(

time: 114 us -> 114 us (level)
  no operation moved by 1% of the time
where the time goes in v5:
time: 114 us
  Pallas kernels  111 us (97%)
  local copies, waits for them, and re-layouts  2.26 us (2%)
    pallas_call x1, Pallas kernels, layer(): pl.pallas_call(layer_kernel, out_shape=jax.ShapeDtypeStruct((NODES, H), B...  111 us

profile of v5, /device:TPU:1, one launch (start us, length us, event | category | flops | bytes accessed | tf_op | source)
XLA Modules:
  0.0 113.6 jit_solution(17811606930509617387)
XLA Ops:
  0.0 111.4 %shard_map.136 = bf16[2048,256]{1,0:T(8,128)(2,1)} custom-call(s32[16,256]{1,0:T(8,128)} %bitcast.9, s32[16,256]{1,0:T(8,128)} %bitcast.10, s32[1,256]{1,0:T(1,128)} %refs_2_.1, bf16[2048,256]{1,0:T(8,128)(2,1)} %refs_3_.1, bf16[256,512]{1,0:T(8,128)(2,1)} %refs_4_.1, f32[1,512]{1,0:T(1,128)} %bitcast.11, bf16[512,256]{1,0:T(8,128)(2,1)} %refs_6_.1, ...), custom_call_target="tpu_custom_call" | custom-call | tf_op jit(solution)/shard_map/pallas_call | solution.py:313
  111.4 2.3 %copy.16 = bf16[2048,256]{1,0:T(8,128)(2,1)} copy(bf16[2048,256]{1,0:T(8,128)(2,1)} %shard_map.136) | data formatting | bytes 2097152
